TPU v7x, 512 devices: a whole 4x4x16 slice. The times are simulated.
512 devices in a mesh: dp: 8 (over x, z_hi), wide: 64 (over y, z_lo, core).
Axes of the slice: x: 4, y: 4, z: 16 (z_hi: 2, z_lo: 8; z = z_hi * 8 + z_lo), core: 2. Of those that a mesh axis runs over, the one named last changes fastest.
Arguments:
- latents: bfloat16 [8, 128, 8, 16, 256], P('dp', 'wide'), may hold values from -36 to 36
- cotangent: bfloat16 [8, 128, 8, 16, 256], P('dp', 'wide'), may hold values from -41 to 41
- norm_gain: float32 [256], replicated, may hold values from 0.25 to 1.75
- norm_bias: float32 [256], replicated, may hold values from -3 to 3
- w_spatial: bfloat16 [2304, 256], P('dp'), may hold values from -0.125 to 0.125
- w_temporal: bfloat16 [768, 256], P('dp'), may hold values from -0.21875 to 0.21875
Outputs:
- block_out: bfloat16 [8, 128, 8, 16, 256], P('dp', 'wide')
- grad_latents: bfloat16 [8, 128, 8, 16, 256], P('dp', 'wide')
- grad_spatial: float32 [2304, 256], P('dp', 'wide')
- grad_temporal: float32 [768, 256], P('dp', 'wide')
- grad_norm: float32 [2, 256], P(None, 'wide')
All inputs are finite; a program needn't handle non-finite values.
Results may differ from a plain program's by a relative error of at most 0.012.
Values may be sent and summed in bfloat16 or wider, within the bound.
A program may use at most 64 MiB of HBM per device.

v0:
```python
import math
import jax
import jax.numpy as jnp
from jax import lax
from jax.sharding import PartitionSpec as P

GROUPS = 32
epsilon = 1e-05


def contract(left, right):
    return lax.dot_general(
        left, right, (((0,), (0,)), ((), ())), preferred_element_type=jnp.float32
    )


def spatial_forward(activated, weights):
    frames, rows_here, cols_here, channels = activated.shape
    padded = jnp.pad(activated, ((0, 0), (1, 1), (1, 1), (0, 0)))
    running = jnp.zeros((frames * rows_here * cols_here, channels), jnp.float32)
    for tap_row in range(3):
        for tap_col in range(3):
            tap_index = 3 * tap_row + tap_col
            window = padded[
                :, tap_row : tap_row + rows_here, tap_col : tap_col + cols_here, :
            ].reshape(-1, channels)
            running = running + jnp.dot(
                window,
                weights[tap_index * channels : (tap_index + 1) * channels],
                preferred_element_type=jnp.float32,
            )
    return running.reshape(frames, rows_here, cols_here, channels)


def spatial_backward(activated, grad_out, weights):
    frames, rows_here, cols_here, channels = activated.shape
    pad_act = jnp.pad(activated, ((0, 0), (1, 1), (1, 1), (0, 0)))
    pad_grad = jnp.pad(grad_out, ((0, 0), (1, 1), (1, 1), (0, 0)))
    flat_grad = grad_out.reshape(-1, channels)
    running = jnp.zeros((frames * rows_here * cols_here, channels), jnp.float32)
    pieces = []
    for tap_row in range(3):
        for tap_col in range(3):
            tap_index = 3 * tap_row + tap_col
            block = weights[tap_index * channels : (tap_index + 1) * channels]
            window_grad = pad_grad[
                :, 2 - tap_row : 2 - tap_row + rows_here, 2 - tap_col : 2 - tap_col + cols_here, :
            ].reshape(-1, channels)
            running = running + jnp.dot(window_grad, block.T, preferred_element_type=jnp.float32)
            window_act = pad_act[
                :, tap_row : tap_row + rows_here, tap_col : tap_col + cols_here, :
            ].reshape(-1, channels)
            pieces.append(contract(window_act, flat_grad))
    return (
        running.reshape(frames, rows_here, cols_here, channels),
        jnp.concatenate(pieces, axis=0),
    )


def temporal_apply(extended, weights, frames):
    channels = extended.shape[-1]
    shape_out = (extended.shape[0], frames, extended.shape[2], channels)
    running = jnp.zeros((shape_out[0] * frames * shape_out[2], channels), jnp.float32)
    for time_delay in range(3):
        earlier = extended[:, 2 - time_delay : 2 - time_delay + frames].reshape(-1, channels)
        running = running + jnp.dot(
            earlier,
            weights[time_delay * channels : (time_delay + 1) * channels],
            preferred_element_type=jnp.float32,
        )
    return running.reshape(shape_out)


def temporal_adjoint(earlier_ext, later_ext, grad_rows, weights):
    frames = grad_rows.shape[1]
    channels = grad_rows.shape[-1]
    flat_grad = grad_rows.reshape(-1, channels)
    running = jnp.zeros(flat_grad.shape, jnp.float32)
    pieces = []
    for time_delay in range(3):
        block = weights[time_delay * channels : (time_delay + 1) * channels]
        later_rows = later_ext[:, time_delay : time_delay + frames].reshape(-1, channels)
        running = running + jnp.dot(later_rows, block.T, preferred_element_type=jnp.float32)
        earlier = earlier_ext[:, 2 - time_delay : 2 - time_delay + frames].reshape(-1, channels)
        pieces.append(contract(earlier, flat_grad))
    return (running.reshape(grad_rows.shape), jnp.concatenate(pieces, axis=0))


def local(latents, cotangent, norm_gain, norm_bias, w_spatial, w_temporal):
    clip_count, frames, rows_here, cols_here, channels = latents.shape
    per_group = channels // GROUPS
    cell_count = rows_here * cols_here
    spatial_full, temporal_full = (
        lax.all_gather(w_spatial, "dp", axis=0, tiled=True),
        lax.all_gather(w_temporal, "dp", axis=0, tiled=True),
    )
    widened = latents.astype(jnp.float32).reshape(
        clip_count, frames, rows_here, cols_here, GROUPS, per_group
    )
    group_sums = jnp.sum(widened, axis=(1, 2, 3, 5))
    squares = jnp.sum(widened * widened, axis=(1, 2, 3, 5))
    total_sums, total_squares = lax.psum((group_sums, squares), "wide")
    cells_count = lax.axis_size("wide") * frames * rows_here * cols_here * per_group
    group_mean = total_sums / cells_count
    variance = total_squares / cells_count - group_mean * group_mean
    inv_std = 1.0 / jnp.sqrt(variance + epsilon)
    mean_wide = group_mean[:, None, None, None, :, None]
    std_wide = inv_std[:, None, None, None, :, None]
    whitened = (widened - mean_wide) * std_wide
    flat_white = whitened.reshape(latents.shape)
    normed = flat_white * norm_gain + norm_bias
    sigmoid = jax.nn.sigmoid(normed)
    activated = (normed * sigmoid).astype(jnp.bfloat16)
    silu_slope = sigmoid * (1.0 + normed * (1.0 - sigmoid))
    stacked = activated.reshape(clip_count * frames, rows_here, cols_here, channels)
    spatial = (
        spatial_forward(stacked, spatial_full)
        .astype(jnp.bfloat16)
        .reshape(clip_count, frames, cell_count, channels)
    )
    grad_rows = cotangent.reshape(clip_count, frames, cell_count, channels)
    row_slab = lax.all_to_all(spatial, "wide", split_axis=2, concat_axis=1, tiled=True)
    extended = jnp.pad(row_slab, ((0, 0), (2, 0), (0, 0), (0, 0)))
    mixed_rows = temporal_apply(extended, temporal_full, row_slab.shape[1])
    returned = lax.all_to_all(
        mixed_rows.astype(jnp.bfloat16), "wide", split_axis=1, concat_axis=2, tiled=True
    ).astype(mixed_rows.dtype)
    grad_slab = lax.all_to_all(grad_rows, "wide", split_axis=2, concat_axis=1, tiled=True)
    earlier_ext = jnp.pad(row_slab, ((0, 0), (2, 0), (0, 0), (0, 0)))
    later_ext = jnp.pad(grad_slab, ((0, 0), (0, 2), (0, 0), (0, 0)))
    slab_wide, local_temporal = temporal_adjoint(earlier_ext, later_ext, grad_slab, temporal_full)
    grad_spatial_act = lax.all_to_all(
        slab_wide.astype(jnp.bfloat16), "wide", split_axis=1, concat_axis=2, tiled=True
    )
    block_out = (latents.astype(jnp.float32) + returned.reshape(latents.shape)).astype(jnp.bfloat16)
    grad_stack = grad_spatial_act.reshape(clip_count * frames, rows_here, cols_here, channels)
    grad_activated, local_spatial = spatial_backward(stacked, grad_stack, spatial_full)
    grad_normed = grad_activated.reshape(latents.shape) * silu_slope
    gain_term = jnp.sum(grad_normed * flat_white, axis=(0, 1, 2, 3))
    bias_term = jnp.sum(grad_normed, axis=(0, 1, 2, 3))
    local_norm = jnp.stack([gain_term, bias_term])
    grad_white = (grad_normed * norm_gain).reshape(widened.shape)
    mean_part = jnp.sum(grad_white, axis=(1, 2, 3, 5))
    cross_part = jnp.sum(grad_white * whitened, axis=(1, 2, 3, 5))
    mean_total, cross_total = lax.psum((mean_part, cross_part), "wide")
    grad_mean = mean_total / cells_count
    grad_cross = cross_total / cells_count
    inner = (
        grad_white
        - grad_mean[:, None, None, None, :, None]
        - whitened * grad_cross[:, None, None, None, :, None]
    ) * std_wide
    grad_latents = (cotangent.astype(jnp.float32) + inner.reshape(latents.shape)).astype(
        jnp.bfloat16
    )
    part_spatial, part_temporal, part_norm = (
        lax.psum_scatter(local_spatial, "wide", scatter_dimension=1, tiled=True),
        lax.psum_scatter(local_temporal, "wide", scatter_dimension=1, tiled=True),
        lax.psum_scatter(local_norm, "wide", scatter_dimension=1, tiled=True),
    )
    summed_spatial, summed_temporal = (
        lax.psum_scatter(
            part_spatial.astype(jnp.bfloat16), "dp", scatter_dimension=0, tiled=True
        ).astype(jnp.float32),
        lax.psum_scatter(
            part_temporal.astype(jnp.bfloat16), "dp", scatter_dimension=0, tiled=True
        ).astype(jnp.float32),
    )
    summed_norm = lax.psum(part_norm, "dp")
    all_cells = (
        clip_count * lax.axis_size("dp") * frames * lax.axis_size("wide") * rows_here * cols_here
    )
    grad_scale = 1.0 / math.sqrt(all_cells)
    return (
        block_out,
        grad_latents,
        summed_spatial * grad_scale,
        summed_temporal * grad_scale,
        summed_norm * grad_scale,
    )


def solution(mesh):
    return jax.shard_map(
        local,
        mesh=mesh,
        in_specs=(
            P("dp", "wide", None, None, None),
            P("dp", "wide", None, None, None),
            P(),
            P(),
            P("dp", None),
            P("dp", None),
        ),
        out_specs=(
            P("dp", "wide", None, None, None),
            P("dp", "wide", None, None, None),
            P("dp", "wide"),
            P("dp", "wide"),
            P(None, "wide"),
        ),
        check_vma=False,
    )
```

profile of v0, /device:TPU:8, one launch (start us, length us, event | category | flops | bytes accessed | tf_op | source)
XLA Modules:
  0.0 1140.6 jit_solution(14482897674854768501)
XLA Ops:
  7.2 0.7 all-gather.2.cloned.1.call-update
  7.9 1.7 copy.53
  9.6 16.2 %all-to-all-start.2 = ((bf16[1,2,128,256]{3,1,0,2:T(2,128)(2,1)}), bf16[1,2,128,256]{3,1,0,2:T(2,128)(2,1)S(1)}, u32[]{:S(2)}, u32[]{:S(2)}) async-start(bf16[1,2,128,256]{3,1,0,2:T(2,128)(2,1)} %bitcast.21), calls=%async_computation.2 | async-start | bytes 262144 | tf_op jit(solution)/shard_map/all_to_all | solution.py:128
  25.8 94.2 %all_gather.7 = bf16[768,256]{1,0:T(8,128)(2,1)S(1)} all-gather(bf16[96,256]{1,0:T(8,128)(2,1)} %param.11), channel_id=1, replica_groups=mesh['dp'=8,'wide'=64] {'dp'}, dimensions={0}, use_global_device_ids=true | all-gather | bytes 442368 | tf_op jit(solution)/shard_map/all_gather | solution.py:95
  120.0 0.6 copy-done.4
  121.8 0.7 convert_element_type.114
  122.5 17.6 %all-to-all-start.3 = ((bf16[1,128,2,256]{3,2,0,1:T(2,128)(2,1)}), bf16[1,128,2,256]{3,2,0,1:T(2,128)(2,1)S(1)}, u32[]{:S(2)}, u32[]{:S(2)}) async-start(bf16[1,128,2,256]{3,2,0,1:T(2,128)(2,1)} %bitcast.25), calls=%async_computation.3 | async-start | bytes 262144 | tf_op jit(solution)/shard_map/all_to_all | solution.py:132
  140.6 198.8 %all-reduce.8 = (f32[1,32]{1,0:T(1,128)S(1)}, f32[1,32]{1,0:T(1,128)S(1)}) all-reduce(f32[1,32]{1,0:T(1,128)S(1)} %bitcast.167, f32[1,32]{1,0:T(1,128)S(1)} %bitcast.166), channel_id=1, replica_groups=mesh['dp'=8,'wide'=64] {'wide'}, use_global_device_ids=true, to_apply=%region_5.6 | all-reduce | flops 64 | bytes 512 | tf_op jit(solution)/shard_map/psum | solution.py:102
  339.8 1.3 dynamic-slice
  342.0 0.8 pad_slice_fusion.12
  343.1 1.2 fusion.53
  344.3 1.1 convolution_add_fusion.7
  347.1 0.8 fusion.24
  347.9 0.6 reduce_sum.104
  348.6 0.6 reduce_sum.100
  349.4 0.9 convolution_dynamic-update-slice_fusion.8
  352.0 0.8 copy.47
  352.8 26.5 %all-to-all-start = ((bf16[1,2,128,256]{3,1,0,2:T(2,128)(2,1)}), bf16[1,2,128,256]{3,1,0,2:T(2,128)(2,1)S(1)}, u32[]{:S(2)}, u32[]{:S(2)}) async-start(bf16[1,2,128,256]{3,1,0,2:T(2,128)(2,1)} %copy.47), calls=%async_computation | async-start | bytes 262144 | tf_op jit(solution)/shard_map/all_to_all | solution.py:122
  379.3 0.9 convolution_dynamic-update-slice_fusion.7
  380.3 0.9 convolution_dynamic-update-slice_fusion.6
  381.2 0.9 convolution_dynamic-update-slice_fusion.5
  382.1 0.9 convolution_dynamic-update-slice_fusion.4
  383.1 0.9 convolution_dynamic-update-slice_fusion.3
  384.0 0.9 convolution_dynamic-update-slice_fusion.2
  384.9 0.9 convolution_dynamic-update-slice_fusion.1
  385.9 0.9 convolution_dynamic-update-slice_fusion
  386.8 6.0 all-to-all-done
  392.8 0.9 convolution_bitcast_fusion
  394.5 0.9 fusion.60
  395.6 0.9 fusion.61
  396.6 0.8 fusion.1
  397.4 1.6 convert_element_type.106
  399.0 1.2 pad_maximum_fusion
  400.2 423.7 %all-reduce.10 = (f32[1,32]{1,0:T(1,128)}, f32[1,32]{1,0:T(1,128)}, bf16[2304,256]{1,0:T(8,128)(2,1)}, bf16[768,256]{1,0:T(8,128)(2,1)}, f32[2,256]{1,0:T(2,128)}) all-reduce(f32[1,32]{1,0:T(1,128)} %bitcast.164, f32[1,32]{1,0:T(1,128)} %bitcast.165, f32[2304,256]{1,0:T(8,128)S(1)} %copy-done.1, ...), channel_id=1, replica_groups=mesh['dp'=8,'wide'=64] {'wide'}, use_global_device_ids=true, to_apply=%region_11.12 | all-reduce | flops 787008 | bytes 4723200 | tf_op jit(solution)/shard_map/psum | solution.py:145
  823.9 0.8 constant_dynamic-slice_fusion
  824.6 44.1 %all-to-all-start.1 = ((bf16[1,128,2,256]{3,2,0,1:T(2,128)(2,1)}), bf16[1,128,2,256]{3,2,0,1:T(2,128)(2,1)S(1)}, u32[]{:S(2)}, u32[]{:S(2)}) async-start(bf16[1,128,2,256]{3,2,0,1:T(2,128)(2,1)} %bitcast.149), calls=%async_computation.1 | async-start | bytes 262144 | tf_op jit(solution)/shard_map/all_to_all | solution.py:125
  868.8 44.0 %psum.39 = f32[2,4]{1,0:T(2,128)S(1)} all-reduce(f32[2,4]{1,0:T(2,128)S(1)} %constant_dynamic-slice_fusion), channel_id=1, replica_groups=mesh['dp'=8,'wide'=64] {'dp'}, use_global_device_ids=true, to_apply=%region_19.20 | all-reduce | flops 8 | bytes 64 | tf_op jit(solution)/shard_map/psum | solution.py:169
  912.8 0.6 broadcast_multiply_fusion
  913.4 1.7 dynamic-slice_convert_fusion.1
  915.1 2.1 dynamic-slice_convert_fusion
  917.7 0.3 reduce-scatter.6.cloned.1.call-update
  918.0 103.3 %reduce-scatter.8.cloned.1.call-done = bf16[96,4]{1,0:T(8,128)(2,1)} async-done(((bf16[768,4]{1,0:T(8,128)(2,1)}), bf16[96,4]{1,0:T(8,128)(2,1)}) %reduce-scatter.8.cloned.1.call-update) | async-done | bytes 784 | tf_op jit(solution)/shard_map/reduce_scatter | solution.py:165
  1021.3 0.7 convert_multiply_fusion.2
  1022.1 0.7 copy.69
  1022.7 108.6 %reduce-scatter.6.cloned.1.call-done = bf16[288,4]{1,0:T(8,128)(2,1)} async-done(((bf16[2304,4]{1,0:T(8,128)(2,1)}), bf16[288,4]{1,0:T(8,128)(2,1)}) %reduce-scatter.6.cloned.1.call-update) | async-done | bytes 2320 | tf_op jit(solution)/shard_map/reduce_scatter | solution.py:162
  1131.3 0.9 convert_multiply_fusion.1
  1132.2 0.7 copy.68
  1133.3 0.8 fusion.23
  (97 shorter events, 7.5 us)
Async XLA Ops:
  7.2 335.9 %all-gather.2.cloned.1.call-start = ((), (), s32[]{:S(2)}) async-start(), calls=%async_computation.6 | async-start | bytes 1327104 | tf_op jit(solution)/shard_map/all_gather | solution.py:94
  9.6 110.4 %all-to-all-start.2 = ((bf16[1,2,128,256]{3,1,0,2:T(2,128)(2,1)}), bf16[1,2,128,256]{3,1,0,2:T(2,128)(2,1)S(1)}, u32[]{:S(2)}, u32[]{:S(2)}) async-start(bf16[1,2,128,256]{3,1,0,2:T(2,128)(2,1)} %bitcast.21), calls=%async_computation.2 | async-start | bytes 262144 | tf_op jit(solution)/shard_map/all_to_all | solution.py:128
  120.0 0.7 copy-start.4
  121.1 19.0 %copy-start.2 = (bf16[1,2,8,16,256]{4,3,2,1,0:T(8,128)(2,1)S(1)}, bf16[1,2,8,16,256]{4,3,2,1,0:T(8,128)(2,1)}, u32[]{:S(2)}) copy-start(bf16[1,2,8,16,256]{4,3,2,1,0:T(8,128)(2,1)} %param.6) | copy-start | bytes 393220
  122.5 219.2 %all-to-all-start.3 = ((bf16[1,128,2,256]{3,2,0,1:T(2,128)(2,1)}), bf16[1,128,2,256]{3,2,0,1:T(2,128)(2,1)S(1)}, u32[]{:S(2)}, u32[]{:S(2)}) async-start(bf16[1,128,2,256]{3,2,0,1:T(2,128)(2,1)} %bitcast.25), calls=%async_computation.3 | async-start | bytes 262144 | tf_op jit(solution)/shard_map/all_to_all | solution.py:132
  343.1 2.4 copy-start
  346.3 0.7 copy-start.6
  346.3 0.7 copy-start.9
  352.8 40.0 %all-to-all-start = ((bf16[1,2,128,256]{3,1,0,2:T(2,128)(2,1)}), bf16[1,2,128,256]{3,1,0,2:T(2,128)(2,1)S(1)}, u32[]{:S(2)}, u32[]{:S(2)}) async-start(bf16[1,2,128,256]{3,1,0,2:T(2,128)(2,1)} %copy.47), calls=%async_computation | async-start | bytes 262144 | tf_op jit(solution)/shard_map/all_to_all | solution.py:122
  383.1 3.8 copy-start.7
  383.1 3.8 copy-start.8
  383.1 9.8 copy-start.5
  396.6 3.6 copy-start.1
  823.9 93.4 %copy-start.10 = (f32[1,32]{1,0:T(1,128)S(1)}, f32[1,32]{1,0:T(1,128)}, u32[]{:S(2)}) copy-start(f32[1,32]{1,0:T(1,128)} %get-tuple-element.31) | copy-start | bytes 388
  823.9 93.4 %copy-start.11 = (f32[1,32]{1,0:T(1,128)S(1)}, f32[1,32]{1,0:T(1,128)}, u32[]{:S(2)}) copy-start(f32[1,32]{1,0:T(1,128)} %get-tuple-element.32) | copy-start | bytes 388
  824.6 308.3 %all-to-all-start.1 = ((bf16[1,128,2,256]{3,2,0,1:T(2,128)(2,1)}), bf16[1,128,2,256]{3,2,0,1:T(2,128)(2,1)S(1)}, u32[]{:S(2)}, u32[]{:S(2)}) async-start(bf16[1,128,2,256]{3,2,0,1:T(2,128)(2,1)} %bitcast.149), calls=%async_computation.1 | async-start | bytes 262144 | tf_op jit(solution)/shard_map/all_to_all | solution.py:125
  868.8 152.5 %reduce-scatter.8.cloned.1.call-start = ((), (), s32[]{:S(2)}) async-start(), calls=%async_computation.8 | async-start | bytes 221184 | tf_op jit(solution)/shard_map/reduce_scatter | solution.py:165
  917.2 214.1 %reduce-scatter.6.cloned.1.call-start = ((), (), s32[]{:S(2)}) async-start(), calls=%async_computation.7 | async-start | bytes 663552 | tf_op jit(solution)/shard_map/reduce_scatter | solution.py:162
  917.7 215.6 %copy-start.3 = (bf16[1,2,8,16,256]{4,3,2,1,0:T(8,128)(2,1)S(1)}, bf16[1,2,8,16,256]{4,3,2,1,0:T(8,128)(2,1)}, u32[]{:S(2)}) copy-start(bf16[1,2,8,16,256]{4,3,2,1,0:T(8,128)(2,1)} %param.7) | copy-start | bytes 393220
Sparse Core Ops, SparseCore 0:
  11.2 113.4 all-gather.1
  917.4 103.9 reduce-scatter.7
  1026.5 104.8 reduce-scatter.5
where the time goes:
time: 1140 us
  blocking collectives  761 us (67%)
  waiting for transfers between devices  219 us (19%)
  starting transfers between devices  105 us (9%)
  matrix products  18.6 us (2%)
  local copies, waits for them, and re-layouts  16.2 us (1%)
  between operations  15 us (1%)
    psum x1, blocking collectives, local(): mean_total, cross_total = lax.psum((mean_part, cross_part), 'wide')  424 us
    psum x1, blocking collectives, local(): total_sums, total_squares = lax.psum((group_sums, squares), 'wide')  199 us
    reduce_scatter x1, waiting for transfers between devices, local(): lax.psum_scatter(part_spatial.astype(jnp.bfloat16), 'dp', scatter_dimensi...  109 us
    reduce_scatter x1, waiting for transfers between devices, local(): lax.psum_scatter(part_temporal.astype(jnp.bfloat16), 'dp', scatter_dimens...  103 us
    all_gather x1, blocking collectives, local(): lax.all_gather(w_temporal, 'dp', axis=0, tiled=True)  94.2 us
    all_to_all x1, starting transfers between devices, local(): lax.all_to_all(mixed_rows.astype(jnp.bfloat16), 'wide', split_axis=1, con...  44.1 us
    psum x1, blocking collectives, local(): summed_norm = lax.psum(part_norm, 'dp')  44 us
    all_to_all x1, starting transfers between devices, local(): lax.all_to_all(spatial, 'wide', split_axis=2, concat_axis=1, tiled=True)  26.5 us
  transfers between devices with their start and end apart: 7, of which 3 were waited for; matrix products, arithmetic and copies ran while one was open for 2% of the time, Pallas kernels for 0%

commit v1 on v0

--- a/solution.py
+++ b/solution.py
@@ -6,6 +6,15 @@
 
 GROUPS = 32
 epsilon = 1e-05
+
+
+def carry_area_in(mine):
+    copies = []
+    for _ in range(lax.axis_size("dp")):
+        copies.append(mine)
+    state_now = jnp.stack(copies, 0)
+    placed = lax.all_to_all(state_now, "dp", 0, 0)
+    return jnp.concatenate(placed, 0)
 
 
 def contract(left, right):
@@ -92,7 +101,7 @@
     cell_count = rows_here * cols_here
     spatial_full, temporal_full = (
         lax.all_gather(w_spatial, "dp", axis=0, tiled=True),
-        lax.all_gather(w_temporal, "dp", axis=0, tiled=True),
+        carry_area_in(w_temporal),
     )
     widened = latents.astype(jnp.float32).reshape(
         clip_count, frames, rows_here, cols_here, GROUPS, per_group

time: 1140 us -> 1090 us (0.956)
  blocking collectives: 761 us -> 701 us
  waiting for transfers between devices: 219 us -> 236 us
  starting transfers between devices: 105 us -> 91.3 us
    all_gather x1 -> x0, blocking collectives: 94.2 us -> none  [local(): lax.all_gather(w_temporal, 'dp', axis=0, tiled=True)]
    all_to_all x0 -> x1, blocking collectives: none -> 29.5 us  [local(): lax.all_to_all(grad_rows, 'wide', split_axis=2, concat_axis=1, tiled=True)]
    all_to_all x1, waiting for transfers between devices: 0.01 us -> 16.5 us  [carry_area_in(): placed = lax.all_to_all(state_now, 'dp', 0, 0)]
  transfers between devices with their start and end apart: 7 -> 7, of which waited for: 3 -> 4; matrix products, arithmetic and copies ran while one was open for 2% -> 2% of each run, Pallas kernels for 0% -> 0%
where the time goes in v1:
time: 1090 us; the launch traced here: 1080 us
  blocking collectives  701 us (64%)
  waiting for transfers between devices  236 us (22%)
  starting transfers between devices  91.3 us (8%)
  matrix products  18.6 us (2%)
  local copies, waits for them, and re-layouts  16.6 us (2%)
  between operations  15 us (1%)
    psum x1, blocking collectives, local(): mean_total, cross_total = lax.psum((mean_part, cross_part), 'wide')  424 us
    psum x1, blocking collectives, local(): total_sums, total_squares = lax.psum((group_sums, squares), 'wide')  210 us
    reduce_scatter x1, waiting for transfers between devices, local(): lax.psum_scatter(part_spatial.astype(jnp.bfloat16), 'dp', scatter_dimensi...  109 us
    reduce_scatter x1, waiting for transfers between devices, local(): lax.psum_scatter(part_temporal.astype(jnp.bfloat16), 'dp', scatter_dimens...  104 us
    all_to_all x1, starting transfers between devices, local(): lax.all_to_all(mixed_rows.astype(jnp.bfloat16), 'wide', split_axis=1, con...  44.1 us
    psum x1, blocking collectives, local(): summed_norm = lax.psum(part_norm, 'dp')  38.5 us
    all_to_all x1, blocking collectives, local(): lax.all_to_all(grad_rows, 'wide', split_axis=2, concat_axis=1, tiled=True)  29.5 us
  transfers between devices with their start and end apart: 7, of which 4 were waited for; matrix products, arithmetic and copies ran while one was open for 2% of the time, Pallas kernels for 0%

profile of v1, /device:TPU:8, one launch (start us, length us, event | category | flops | bytes accessed | tf_op | source)
XLA Modules:
  0.0 1084.9 jit_solution(2755297312431815587)
XLA Ops:
  7.2 1.0 copy.53
  8.2 29.5 %all_to_all.65 = bf16[1,2,128,256]{3,1,0,2:T(2,128)(2,1)S(1)} all-to-all(bf16[1,2,128,256]{3,1,0,2:T(2,128)(2,1)S(1)} %bitcast.160), channel_id=1, replica_groups=mesh['dp'=8,'wide'=64] {'wide'}, dimensions={2} | all-to-all | bytes 262144 | tf_op jit(solution)/shard_map/all_to_all | solution.py:137
  37.7 1.6 stack.8
  39.3 10.0 all-to-all-start.1
  49.4 0.7 all-gather.2.cloned.1.call-update
  50.6 16.5 %all-to-all-done.1 = bf16[8,96,256]{2,1,0:T(8,128)(2,1)S(1)} async-done(((bf16[8,96,256]{2,1,0:T(8,128)(2,1)}), bf16[8,96,256]{2,1,0:T(8,128)(2,1)S(1)}, u32[]{:S(2)}, u32[]{:S(2)}) %all-to-all-start.1) | async-done | bytes 393248 | tf_op jit(solution)/shard_map/all_to_all | solution.py:16
  67.8 0.7 convert_element_type.114
  68.5 18.6 %all-to-all-start.4 = ((bf16[1,128,2,256]{3,2,0,1:T(2,128)(2,1)}), bf16[1,128,2,256]{3,2,0,1:T(2,128)(2,1)S(1)}, u32[]{:S(2)}, u32[]{:S(2)}) async-start(bf16[1,128,2,256]{3,2,0,1:T(2,128)(2,1)} %bitcast.26), calls=%async_computation.4 | async-start | bytes 262144 | tf_op jit(solution)/shard_map/all_to_all | solution.py:141
  87.6 209.5 %all-reduce.8 = (f32[1,32]{1,0:T(1,128)S(1)}, f32[1,32]{1,0:T(1,128)S(1)}) all-reduce(f32[1,32]{1,0:T(1,128)S(1)} %bitcast.175, f32[1,32]{1,0:T(1,128)S(1)} %bitcast.174), channel_id=1, replica_groups=mesh['dp'=8,'wide'=64] {'wide'}, use_global_device_ids=true, to_apply=%region_5.6 | all-reduce | flops 64 | bytes 512 | tf_op jit(solution)/shard_map/psum | solution.py:111
  297.5 1.3 dynamic-slice
  299.7 0.8 pad_slice_fusion.12
  300.8 1.2 fusion.53
  302.0 1.1 convolution_add_fusion.7
  304.8 0.8 fusion.24
  305.6 0.6 reduce_sum.104
  306.4 0.6 reduce_sum.100
  307.1 0.9 convolution_dynamic-update-slice_fusion.8
  309.7 0.8 copy.47
  310.5 18.4 %all-to-all-start = ((bf16[1,2,128,256]{3,1,0,2:T(2,128)(2,1)}), bf16[1,2,128,256]{3,1,0,2:T(2,128)(2,1)S(1)}, u32[]{:S(2)}, u32[]{:S(2)}) async-start(bf16[1,2,128,256]{3,1,0,2:T(2,128)(2,1)} %copy.47), calls=%async_computation | async-start | bytes 262144 | tf_op jit(solution)/shard_map/all_to_all | solution.py:131
  329.0 0.9 convolution_dynamic-update-slice_fusion.7
  329.9 0.9 convolution_dynamic-update-slice_fusion.6
  330.8 0.9 convolution_dynamic-update-slice_fusion.5
  331.7 0.9 convolution_dynamic-update-slice_fusion.4
  332.7 0.9 convolution_dynamic-update-slice_fusion.3
  333.6 0.9 convolution_dynamic-update-slice_fusion.2
  334.6 0.9 convolution_dynamic-update-slice_fusion.1
  335.5 0.9 convolution_dynamic-update-slice_fusion
  336.5 6.0 all-to-all-done
  342.5 0.9 convolution_bitcast_fusion
  344.1 0.9 fusion.60
  345.2 0.9 fusion.61
  346.2 0.8 fusion.1
  347.0 1.6 convert_element_type.106
  348.6 1.2 pad_maximum_fusion
  349.8 423.6 %all-reduce.10 = (f32[1,32]{1,0:T(1,128)}, f32[1,32]{1,0:T(1,128)}, bf16[2304,256]{1,0:T(8,128)(2,1)}, bf16[768,256]{1,0:T(8,128)(2,1)}, f32[2,256]{1,0:T(2,128)}) all-reduce(f32[1,32]{1,0:T(1,128)} %bitcast.172, f32[1,32]{1,0:T(1,128)} %bitcast.173, f32[2304,256]{1,0:T(8,128)S(1)} %copy-done.1, ...), channel_id=1, replica_groups=mesh['dp'=8,'wide'=64] {'wide'}, use_global_device_ids=true, to_apply=%region_11.12 | all-reduce | flops 787008 | bytes 4723200 | tf_op jit(solution)/shard_map/psum | solution.py:154
  773.4 0.8 constant_dynamic-slice_fusion
  774.2 44.1 %all-to-all-start.2 = ((bf16[1,128,2,256]{3,2,0,1:T(2,128)(2,1)}), bf16[1,128,2,256]{3,2,0,1:T(2,128)(2,1)S(1)}, u32[]{:S(2)}, u32[]{:S(2)}) async-start(bf16[1,128,2,256]{3,2,0,1:T(2,128)(2,1)} %bitcast.156), calls=%async_computation.2 | async-start | bytes 262144 | tf_op jit(solution)/shard_map/all_to_all | solution.py:134
  818.4 38.5 %psum.39 = f32[2,4]{1,0:T(2,128)S(1)} all-reduce(f32[2,4]{1,0:T(2,128)S(1)} %constant_dynamic-slice_fusion), channel_id=1, replica_groups=mesh['dp'=8,'wide'=64] {'dp'}, use_global_device_ids=true, to_apply=%region_19.20 | all-reduce | flops 8 | bytes 64 | tf_op jit(solution)/shard_map/psum | solution.py:178
  856.9 0.6 broadcast_multiply_fusion
  857.4 1.7 dynamic-slice_convert_fusion.1
  859.2 2.1 dynamic-slice_convert_fusion
  862.1 103.6 %reduce-scatter.8.cloned.1.call-done = bf16[96,4]{1,0:T(8,128)(2,1)} async-done(((bf16[768,4]{1,0:T(8,128)(2,1)}), bf16[96,4]{1,0:T(8,128)(2,1)}) %reduce-scatter.8.cloned.1.call-update) | async-done | bytes 784 | tf_op jit(solution)/shard_map/reduce_scatter | solution.py:174
  965.6 0.7 convert_multiply_fusion.2
  966.4 0.7 copy.69
  967.0 108.6 %reduce-scatter.6.cloned.1.call-done = bf16[288,4]{1,0:T(8,128)(2,1)} async-done(((bf16[2304,4]{1,0:T(8,128)(2,1)}), bf16[288,4]{1,0:T(8,128)(2,1)}) %reduce-scatter.6.cloned.1.call-update) | async-done | bytes 2320 | tf_op jit(solution)/shard_map/reduce_scatter | solution.py:171
  1075.6 0.9 convert_multiply_fusion.1
  1076.5 0.7 copy.68
  1077.6 0.8 fusion.23
  (98 shorter events, 7.8 us)
Async XLA Ops:
  37.7 12.4 %copy-start.4 = (bf16[1,2,128,256]{3,1,0,2:T(2,128)(2,1)}, bf16[1,2,128,256]{3,1,0,2:T(2,128)(2,1)S(1)}, u32[]{:S(2)}) copy-start(bf16[1,2,128,256]{3,1,0,2:T(2,128)(2,1)S(1)} %all_to_all.65) | copy-start | bytes 393220
  39.3 27.8 %all-to-all-start.1 = ((bf16[8,96,256]{2,1,0:T(8,128)(2,1)}), bf16[8,96,256]{2,1,0:T(8,128)(2,1)S(1)}, u32[]{:S(2)}, u32[]{:S(2)}) async-start(bf16[8,96,256]{2,1,0:T(8,128)(2,1)} %stack.8), calls=%async_computation.1 | async-start | bytes 786432 | tf_op jit(solution)/shard_map/all_to_all | solution.py:16
  49.3 251.4 %all-gather.2.cloned.1.call-start = ((), (), s32[]{:S(2)}) async-start(), calls=%async_computation.7 | async-start | bytes 1327104 | tf_op jit(solution)/shard_map/all_gather | solution.py:103
  67.1 20.0 %copy-start.2 = (bf16[1,2,8,16,256]{4,3,2,1,0:T(8,128)(2,1)S(1)}, bf16[1,2,8,16,256]{4,3,2,1,0:T(8,128)(2,1)}, u32[]{:S(2)}) copy-start(bf16[1,2,8,16,256]{4,3,2,1,0:T(8,128)(2,1)} %param.6) | copy-start | bytes 393220
  68.5 230.9 %all-to-all-start.4 = ((bf16[1,128,2,256]{3,2,0,1:T(2,128)(2,1)}), bf16[1,128,2,256]{3,2,0,1:T(2,128)(2,1)S(1)}, u32[]{:S(2)}, u32[]{:S(2)}) async-start(bf16[1,128,2,256]{3,2,0,1:T(2,128)(2,1)} %bitcast.26), calls=%async_computation.4 | async-start | bytes 262144 | tf_op jit(solution)/shard_map/all_to_all | solution.py:141
  300.8 2.4 copy-start
  304.0 0.7 copy-start.6
  304.1 0.7 copy-start.9
  310.5 31.9 %all-to-all-start = ((bf16[1,2,128,256]{3,1,0,2:T(2,128)(2,1)}), bf16[1,2,128,256]{3,1,0,2:T(2,128)(2,1)S(1)}, u32[]{:S(2)}, u32[]{:S(2)}) async-start(bf16[1,2,128,256]{3,1,0,2:T(2,128)(2,1)} %copy.47), calls=%async_computation | async-start | bytes 262144 | tf_op jit(solution)/shard_map/all_to_all | solution.py:131
  332.7 3.8 copy-start.7
  332.7 3.8 copy-start.8
  332.7 9.8 copy-start.5
  346.2 3.6 copy-start.1
  773.4 87.9 %copy-start.10 = (f32[1,32]{1,0:T(1,128)S(1)}, f32[1,32]{1,0:T(1,128)}, u32[]{:S(2)}) copy-start(f32[1,32]{1,0:T(1,128)} %get-tuple-element.31) | copy-start | bytes 388
  773.4 87.9 %copy-start.11 = (f32[1,32]{1,0:T(1,128)S(1)}, f32[1,32]{1,0:T(1,128)}, u32[]{:S(2)}) copy-start(f32[1,32]{1,0:T(1,128)} %get-tuple-element.32) | copy-start | bytes 388
  774.2 303.0 %all-to-all-start.2 = ((bf16[1,128,2,256]{3,2,0,1:T(2,128)(2,1)}), bf16[1,128,2,256]{3,2,0,1:T(2,128)(2,1)S(1)}, u32[]{:S(2)}, u32[]{:S(2)}) async-start(bf16[1,128,2,256]{3,2,0,1:T(2,128)(2,1)} %bitcast.156), calls=%async_computation.2 | async-start | bytes 262144 | tf_op jit(solution)/shard_map/all_to_all | solution.py:134
  818.3 147.3 %reduce-scatter.8.cloned.1.call-start = ((), (), s32[]{:S(2)}) async-start(), calls=%async_computation.9 | async-start | bytes 221184 | tf_op jit(solution)/shard_map/reduce_scatter | solution.py:174
  861.3 214.3 %reduce-scatter.6.cloned.1.call-start = ((), (), s32[]{:S(2)}) async-start(), calls=%async_computation.8 | async-start | bytes 663552 | tf_op jit(solution)/shard_map/reduce_scatter | solution.py:171
  861.7 215.8 %copy-start.3 = (bf16[1,2,8,16,256]{4,3,2,1,0:T(8,128)(2,1)S(1)}, bf16[1,2,8,16,256]{4,3,2,1,0:T(8,128)(2,1)}, u32[]{:S(2)}) copy-start(bf16[1,2,8,16,256]{4,3,2,1,0:T(8,128)(2,1)} %param.7) | copy-start | bytes 393220
Sparse Core Ops, SparseCore 0:
  53.4 95.4 all-gather.1
  861.4 104.1 reduce-scatter.7
  970.8 104.8 reduce-scatter.5
